TPU v7x, 32 devices: a whole 2x2x4 slice. The times are simulated.
32 devices in a mesh: rows: 4 (over y, x), cols: 8 (over z, core).
Axes of the slice: x: 2, y: 2, z: 4, core: 2. Of those that a mesh axis runs over, the one named last changes fastest.
Arguments:
- sensitivity: bfloat16 [4, 32, 512, 512], P('rows', 'cols'), may hold values from -0.25 to 0.25
- tile_rows: int32 [4, 32], P('rows', 'cols'), may hold values from 0 to 127, as said below
- tile_cols: int32 [4, 32], P('rows', 'cols'), may hold values from 0 to 1, as said below
- kept_counts: int32 [4, 32], P('rows', 'cols'), may hold values from 0 to 512, as said below
- misfit: float32 [262144], P('rows'), may hold values from -6 to 6
- data_weight: float32 [262144], P('rows'), may hold values from 0.3 to 3
- depth_weight: float32 [8192], P('cols'), may hold values from 0.25 to 3
- density: float32 [8192], P('cols'), may hold values from -6 to 6
Outputs:
- new_density: float32 [8192], P('cols')
- new_misfit: float32 [262144], P(('rows', 'cols'))
Inputs may be any that keep to these rules, and one draw needn't show every extreme that they name: Within the 4 slots of one device the pairs (tile_rows, tile_cols) are distinct. Within the 4 slots of one device the pairs (tile_rows, tile_cols) are distinct. A slot with kept_counts 0 is empty, and empty slots come after all live slots of a device; a live slot keeps 512 // 2 or more coefficients; every device has a live slot, and some device has all 4 slots live.
All inputs are finite; a program needn't handle non-finite values.
Results may differ from a plain program's by a relative error of at most 0.033.
Values may be sent and summed in bfloat16 or wider, within the bound.
A program may use at most 64 MiB of HBM per device.

v0:
```python
import math

import jax
import jax.numpy as jnp
from jax import lax
from jax.sharding import PartitionSpec as P

ITERS = 4


damping = 1.0


def haar_matrix(tile_size):
    rows_index = jnp.arange(tile_size, dtype=jnp.int32)[:, None]
    column_index = jnp.arange(tile_size, dtype=jnp.int32)[None, :]
    levels = jnp.zeros_like(rows_index)
    for bit_shift in range(1, tile_size.bit_length()):
        levels = levels + (rows_index >= 1 << bit_shift).astype(jnp.int32)
    support = jnp.right_shift(tile_size, levels)
    offset = (rows_index - jnp.left_shift(1, levels)) * support
    inside = (column_index >= offset) & (column_index < offset + support)
    polarity = jnp.where(column_index < offset + support // 2, 1.0, -1.0)
    detail = jnp.where(inside, polarity, 0.0) / jnp.sqrt(support.astype(jnp.float32))
    coarse = jnp.full((1, tile_size), 1.0 / math.sqrt(tile_size), jnp.float32)
    return jnp.concatenate([coarse, detail[1:]], axis=0)


def squared_norm(values):
    return lax.psum(jnp.sum(values * values), "cols")


def per_device(
    sensitivity, tile_rows, tile_cols, kept_counts, misfit, data_weight, depth_weight, density
):
    tile_stack = sensitivity[0]
    slot_rows = tile_rows[0]
    slot_cols = tile_cols[0]
    slot_kept = kept_counts[0]
    tile_size = tile_stack.shape[-1]
    data_blocks = misfit.shape[0] // tile_size
    model_blocks = density.shape[0] // tile_size
    wavelet = haar_matrix(tile_size)
    coefficient_index = jnp.arange(tile_size, dtype=jnp.int32)
    live_mask = coefficient_index[None, :] < slot_kept[:, None]
    pick_rows = slot_rows[:, None] == jnp.arange(data_blocks, dtype=jnp.int32)[None, :]
    pick_cols = slot_cols[:, None] == jnp.arange(model_blocks, dtype=jnp.int32)[None, :]
    share_len = misfit.shape[0] // lax.axis_size("cols")
    share_start = lax.axis_index("cols") * share_len
    squared = data_weight * data_weight

    def adjoint_part(weighted):
        data_rows = weighted.reshape(data_blocks, tile_size)
        picked = jnp.dot(
            pick_rows.astype(jnp.bfloat16), data_rows, preferred_element_type=jnp.float32
        ).astype(jnp.bfloat16)
        products = jnp.einsum("sab,sa->sb", tile_stack, picked, preferred_element_type=jnp.float32)
        products = jnp.where(live_mask, products, 0.0)
        block_sums = jnp.dot(
            pick_cols.T.astype(jnp.float32), products, precision=lax.Precision.HIGHEST
        )
        cell_part = jnp.dot(block_sums, wavelet, precision=lax.Precision.HIGHEST).reshape(-1)
        return lax.psum(cell_part, "rows")

    rhs = depth_weight * adjoint_part((squared * misfit).astype(jnp.bfloat16)) - damping * density
    solution = jnp.zeros_like(density)
    residual = rhs
    direction = rhs
    norm_now = squared_norm(residual)
    change = jnp.zeros_like(misfit)
    for iteration in range(ITERS):
        coeffs = jnp.dot(
            (depth_weight * direction).reshape(model_blocks, tile_size),
            wavelet.T,
            precision=lax.Precision.HIGHEST,
        )
        forward_picked = jnp.dot(
            pick_cols.astype(jnp.float32), coeffs, precision=lax.Precision.HIGHEST
        )
        forward_picked = jnp.where(live_mask, forward_picked, 0.0).astype(jnp.bfloat16)
        forward_products = jnp.einsum(
            "sab,sb->sa", tile_stack, forward_picked, preferred_element_type=jnp.float32
        )
        summed = jnp.dot(
            pick_rows.T.astype(jnp.float32), forward_products, precision=lax.Precision.HIGHEST
        )
        partial_data = summed.reshape(-1)
        image_data = lax.psum(partial_data, "cols")
        weighted = (squared * image_data).astype(jnp.bfloat16)
        image_cells = depth_weight * adjoint_part(weighted) + damping * direction
        curvature_sum, cross_sum, image_sum = lax.psum(
            (
                jnp.sum(direction * image_cells),
                jnp.sum(residual * image_cells),
                jnp.sum(image_cells * image_cells),
            ),
            "cols",
        )
        step_length = norm_now / curvature_sum
        solution = solution + step_length * direction
        residual = residual - step_length * image_cells
        change = change + step_length * image_data
        if iteration + 1 < ITERS:
            norm_next = (
                norm_now - 2.0 * step_length * cross_sum + step_length * step_length * image_sum
            )
            direction = residual + norm_next / norm_now * direction
            norm_now = norm_next
    new_density = density + depth_weight * solution
    new_misfit = lax.dynamic_slice_in_dim(misfit - change, share_start, share_len)
    return (new_density, new_misfit)


def solution(mesh):
    return jax.shard_map(
        per_device,
        mesh=mesh,
        in_specs=(
            P("rows", "cols", None, None),
            P("rows", "cols"),
            P("rows", "cols"),
            P("rows", "cols"),
            P("rows"),
            P("rows"),
            P("cols"),
            P("cols"),
        ),
        out_specs=(P("cols"), P(("rows", "cols"))),
        check_vma=False,
    )
```

profile of v0, /device:TPU:0, one launch (start us, length us, event | category | flops | bytes accessed | tf_op | source)
XLA Modules:
  0.0 381.1 jit_solution(3259182382915004506)
XLA Ops:
  7.3 1.2 multiply_convert_fusion.4
  11.4 11.4 %psum.136 = f32[1024]{0:T(1024)S(1)} all-reduce(f32[1024]{0:T(1024)S(1)} %bitcast.116), channel_id=1, replica_groups=mesh['rows'=4,'cols'=8] {'rows'}, use_global_device_ids=true, to_apply=%region_0.1 | all-reduce | flops 1024 | bytes 8192 | tf_op jit(solution)/shard_map/psum | solution.py:63
  25.9 54.9 %all-reduce.9.cloned.1.call-done = f32[65536]{0:T(1024)} async-done(((f32[65536]{0:T(1024)}), f32[65536]{0:T(1024)}) %all-reduce.9.cloned.1.call-update) | async-done | bytes 262160 | tf_op jit(solution)/shard_map/psum | solution.py:88
  80.8 1.0 multiply_convert_fusion.3
  82.5 1.1 fusion.23
  85.6 9.8 %psum.139 = f32[1024]{0:T(1024)S(1)} all-reduce(f32[1024]{0:T(1024)S(1)} %bitcast.117), channel_id=1, replica_groups=mesh['rows'=4,'cols'=8] {'rows'}, use_global_device_ids=true, to_apply=%region_4.5 | all-reduce | flops 1024 | bytes 8192 | tf_op jit(solution)/shard_map/psum | solution.py:63
  96.1 14.3 %all-reduce.3 = (f32[]{:T(128)}, f32[]{:T(128)}, f32[]{:T(128)}) all-reduce(f32[]{:T(128)} %get-tuple-element.10, f32[]{:T(128)} %get-tuple-element.9, f32[]{:T(128)} %get-tuple-element.8), channel_id=1, replica_groups=mesh['rows'=4,'cols'=8] {'cols'}, use_global_device_ids=true, to_apply=%region_2.3 | all-reduce | flops 3 | bytes 24 | tf_op jit(solution)/shard_map/psum | solution.py:30
  117.4 51.9 %all-reduce.11.cloned.1.call-done = f32[65536]{0:T(1024)} async-done(((f32[65536]{0:T(1024)}), f32[65536]{0:T(1024)}) %all-reduce.11.cloned.1.call-update) | async-done | bytes 262160 | tf_op jit(solution)/shard_map/psum | solution.py:88
  169.3 1.0 multiply_convert_fusion.2
  171.0 1.1 fusion.24
  174.1 9.8 %psum.143 = f32[1024]{0:T(1024)S(1)} all-reduce(f32[1024]{0:T(1024)S(1)} %bitcast.118), channel_id=1, replica_groups=mesh['rows'=4,'cols'=8] {'rows'}, use_global_device_ids=true, to_apply=%region_10.11 | all-reduce | flops 1024 | bytes 8192 | tf_op jit(solution)/shard_map/psum | solution.py:63
  184.6 14.3 %all-reduce.2 = (f32[]{:T(128)}, f32[]{:T(128)}, f32[]{:T(128)}) all-reduce(f32[]{:T(128)} %get-tuple-element.7, f32[]{:T(128)} %get-tuple-element.6, f32[]{:T(128)} %get-tuple-element.5), channel_id=1, replica_groups=mesh['rows'=4,'cols'=8] {'cols'}, use_global_device_ids=true, to_apply=%region_12.13 | all-reduce | flops 3 | bytes 24 | tf_op jit(solution)/shard_map/psum | solution.py:91
  204.0 51.9 %all-reduce.13.cloned.1.call-done = f32[65536]{0:T(1024)} async-done(((f32[65536]{0:T(1024)}), f32[65536]{0:T(1024)}) %all-reduce.13.cloned.1.call-update) | async-done | bytes 262160 | tf_op jit(solution)/shard_map/psum | solution.py:88
  255.8 1.0 multiply_convert_fusion.1
  257.6 1.1 fusion.25
  260.0 9.8 %psum.148 = f32[1024]{0:T(1024)S(1)} all-reduce(f32[1024]{0:T(1024)S(1)} %bitcast.119), channel_id=1, replica_groups=mesh['rows'=4,'cols'=8] {'rows'}, use_global_device_ids=true, to_apply=%region_18.19 | all-reduce | flops 1024 | bytes 8192 | tf_op jit(solution)/shard_map/psum | solution.py:63
  270.5 14.3 %all-reduce.1 = (f32[]{:T(128)}, f32[]{:T(128)}, f32[]{:T(128)}) all-reduce(f32[]{:T(128)} %get-tuple-element.4, f32[]{:T(128)} %get-tuple-element.3, f32[]{:T(128)} %get-tuple-element.2), channel_id=1, replica_groups=mesh['rows'=4,'cols'=8] {'cols'}, use_global_device_ids=true, to_apply=%region_20.21 | all-reduce | flops 3 | bytes 24 | tf_op jit(solution)/shard_map/psum | solution.py:91
  289.9 51.9 %all-reduce.15.cloned.1.call-done = f32[65536]{0:T(1024)} async-done(((f32[65536]{0:T(1024)}), f32[65536]{0:T(1024)}) %all-reduce.15.cloned.1.call-update) | async-done | bytes 262160 | tf_op jit(solution)/shard_map/psum | solution.py:88
  341.8 1.0 multiply_convert_fusion
  345.7 9.8 %psum.153 = f32[1024]{0:T(1024)S(1)} all-reduce(f32[1024]{0:T(1024)S(1)} %bitcast.120), channel_id=1, replica_groups=mesh['rows'=4,'cols'=8] {'rows'}, use_global_device_ids=true, to_apply=%region_26.27 | all-reduce | flops 1024 | bytes 8192 | tf_op jit(solution)/shard_map/psum | solution.py:63
  355.6 1.3 fusion.75
  356.9 14.3 %psum.154 = f32[]{:T(128)} all-reduce(f32[]{:T(128)} %fusion.75), channel_id=1, replica_groups=mesh['rows'=4,'cols'=8] {'cols'}, use_global_device_ids=true, to_apply=%region_28.29 | all-reduce | flops 1 | bytes 8 | tf_op jit(solution)/shard_map/psum | solution.py:91
  371.8 1.3 multiply_add_fusion
  373.2 1.4 dynamic-slice_subtract_fusion
  (107 shorter events, 27.8 us)
Async XLA Ops:
  7.2 2.6 copy-start
  7.2 2.9 copy-start.12
  7.2 2.9 copy-start.8
  7.2 73.6 %all-reduce.9.cloned.1.call-start = ((), (), s32[]{:S(2)}) async-start(), calls=%async_computation | async-start | bytes 524288 | tf_op jit(solution)/shard_map/psum | solution.py:88
  9.7 13.1 %copy-start.2 = (f32[1024]{0:T(1024)S(1)}, f32[1024]{0:T(1024)}, u32[]{:S(2)}) copy-start(f32[1024]{0:T(1024)} %param.14) | copy-start | bytes 12292
  9.7 13.1 %copy-start.4 = (f32[1024]{0:T(1024)S(1)}, f32[1024]{0:T(1024)}, u32[]{:S(2)}) copy-start(f32[1024]{0:T(1024)} %param.15) | copy-start | bytes 12292
  10.8 13.9 %copy-start.5 = (s32[1,4]{1,0:T(1,128)S(1)}, s32[1,4]{1,0:T(1,128)}, u32[]{:S(2)}) copy-start(s32[1,4]{1,0:T(1,128)} %param.9) | copy-start | bytes 52
  22.8 58.0 %copy-start.1 = (f32[65536]{0:T(1024)S(1)}, f32[65536]{0:T(1024)}, u32[]{:S(2)}) copy-start(f32[65536]{0:T(1024)} %param.13) | copy-start | bytes 786436
  25.9 143.4 %all-reduce.11.cloned.1.call-start = ((), (), s32[]{:S(2)}) async-start(), calls=%async_computation.1 | async-start | bytes 524288 | tf_op jit(solution)/shard_map/psum | solution.py:88
  83.6 31.7 %copy-start.9 = (s32[1,4]{1,0:T(1,128)S(1)}, s32[1,4]{1,0:T(1,128)}, u32[]{:S(2)}) copy-start(s32[1,4]{1,0:T(1,128)} %param.11) | copy-start | bytes 52
  83.6 31.7 %copy-start.13 = (s32[1,4]{1,0:T(1,128)S(1)}, s32[1,4]{1,0:T(1,128)}, u32[]{:S(2)}) copy-start(s32[1,4]{1,0:T(1,128)} %param.10) | copy-start | bytes 52
  117.4 138.4 %all-reduce.13.cloned.1.call-start = ((), (), s32[]{:S(2)}) async-start(), calls=%async_computation.2 | async-start | bytes 524288 | tf_op jit(solution)/shard_map/psum | solution.py:88
  172.1 29.7 %copy-start.10 = (s32[1,4]{1,0:T(1,128)S(1)}, s32[1,4]{1,0:T(1,128)}, u32[]{:S(2)}) copy-start(s32[1,4]{1,0:T(1,128)} %param.11) | copy-start | bytes 52
  172.1 29.7 %copy-start.14 = (s32[1,4]{1,0:T(1,128)S(1)}, s32[1,4]{1,0:T(1,128)}, u32[]{:S(2)}) copy-start(s32[1,4]{1,0:T(1,128)} %param.10) | copy-start | bytes 52
  173.4 29.3 %copy-start.6 = (s32[1,4]{1,0:T(1,128)S(1)}, s32[1,4]{1,0:T(1,128)}, u32[]{:S(2)}) copy-start(s32[1,4]{1,0:T(1,128)} %param.9) | copy-start | bytes 52
  203.9 137.9 %all-reduce.15.cloned.1.call-start = ((), (), s32[]{:S(2)}) async-start(), calls=%async_computation.3 | async-start | bytes 524288 | tf_op jit(solution)/shard_map/psum | solution.py:88
  257.5 1.5 copy-start.11
  257.5 1.5 copy-start.15
  259.3 29.4 %copy-start.7 = (s32[1,4]{1,0:T(1,128)S(1)}, s32[1,4]{1,0:T(1,128)}, u32[]{:S(2)}) copy-start(s32[1,4]{1,0:T(1,128)} %param.9) | copy-start | bytes 52
  269.8 20.1 %copy-start.3 = (f32[1024]{0:T(1024)}, f32[1024]{0:T(1024)S(1)}, u32[]{:S(2)}) copy-start(f32[1024]{0:T(1024)S(1)} %psum.148) | copy-start | bytes 12292
Sparse Core Ops, SparseCore 0:
  26.0 54.7 all-reduce.8
  117.5 51.7 all-reduce.10
  204.0 51.7 all-reduce.12
  290.0 51.7 all-reduce.14
where the time goes:
time: 382 us; the launch traced here: 381 us
  waiting for transfers between devices  211 us (55%)
  blocking collectives  108 us (28%)
  between operations  22.5 us (6%)
  matrix products  22.4 us (6%)
  other arithmetic  11.7 us (3%)
  local copies, waits for them, and re-layouts  5.95 us (2%)
    psum x4, waiting for transfers between devices, per_device(): image_data = lax.psum(partial_data, 'cols')  211 us
    psum x5, blocking collectives, adjoint_part(): return lax.psum(cell_part, 'rows')  50.7 us
    psum x3, blocking collectives, per_device(): lax.psum((jnp.sum(direction * image_cells), jnp.sum(residual * image_cell...  42.9 us
    psum x1, blocking collectives, squared_norm(): return lax.psum(jnp.sum(values * values), 'cols')  14.3 us
  transfers between devices with their start and end apart: 4, of which 4 were waited for; matrix products, arithmetic and copies ran while one was open for 0% of the time, Pallas kernels for 0%

commit v1 on v0

v1 whole, which is shorter than its diff:
```python
import functools
import math

import jax
import jax.numpy as jnp
import numpy as np
from jax import lax
from jax.experimental import pallas as pl
from jax.experimental.pallas import tpu as pltpu
from jax.sharding import PartitionSpec as P

ITERS = 4
DAMPING = 1.0
LANES = 128
F32 = jnp.float32
BF16 = jnp.bfloat16


def haar_signs(size):
    signs = np.zeros((size, size), np.float32)
    scale = np.zeros((1, size), np.float32)
    signs[0] = 1.0
    scale[0, 0] = 1.0 / math.sqrt(size)
    for n in range(1, size):
        level = n.bit_length() - 1
        k = n - (1 << level)
        support = size >> level
        signs[n, k * support : k * support + support // 2] = 1.0
        signs[n, k * support + support // 2 : (k + 1) * support] = -1.0
        scale[0, n] = 1.0 / math.sqrt(support)
    return signs, scale


def split3(x):
    hi = x.astype(BF16)
    rest = x - hi.astype(F32)
    mid = rest.astype(BF16)
    low = (rest - mid.astype(F32)).astype(BF16)
    return hi, mid, low


def nn(a, b):
    return lax.dot_general(a, b, (((1,), (0,)), ((), ())), preferred_element_type=F32)


def nt(a, b):
    return lax.dot_general(a, b, (((1,), (1,)), ((), ())), preferred_element_type=F32)


def select_dot(sel, x):
    hi, mid, low = split3(x)
    return nn(sel, hi) + (nn(sel, mid) + nn(sel, low))


def to_rows(x, width):
    q = width // LANES
    return [
        jnp.concatenate([x[i * q + j : i * q + j + 1, :] for j in range(q)], axis=1)
        for i in range(x.shape[0] // q)
    ]


def to_lanes(rows):
    q = rows[0].shape[1] // LANES
    return jnp.concatenate(
        [row[:, j * LANES : (j + 1) * LANES] for row in rows for j in range(q)], axis=0
    )


def haar_apply(dot, rows, matrix):
    m = len(rows)
    parts = [split3(row) for row in rows]
    lhs = jnp.concatenate([p[t].astype(F32) for t in range(3) for p in parts], axis=0).astype(BF16)
    out = dot(lhs, matrix)
    return [out[i : i + 1] + (out[m + i : m + i + 1] + out[2 * m + i : 2 * m + i + 1]) for i in range(m)]


def total(rows):
    acc = rows[0]
    for row in rows[1:]:
        acc = acc + row
    return jnp.sum(acc, axis=1, keepdims=True)


def kernel(
    n_rows, n_cols, slots,
    rows_s, cols_s, kept_s, scale_ref, depth_ref, density_ref,
    tiles_hbm, signs_hbm, misfit_hbm, weight_hbm,
    density_out, misfit_out,
    tiles, signs, misfit, weight,
    idbuf, colbuf, rowbuf, curvbuf, image_ref, match_ref,
    load_sem, id_send, id_recv, col_send, col_recv, row_send, row_recv, curv_send, curv_recv,
):
    size = tiles.shape[-1]
    q = size // LANES
    blocks = depth_ref.shape[0] * LANES // size
    mrows = slots * q
    n = n_cols * mrows
    me_r = lax.axis_index("rows")
    me_c = lax.axis_index("cols")

    loads = [
        pltpu.make_async_copy(src, dst, load_sem.at[i])
        for i, (src, dst) in enumerate(
            ((weight_hbm, weight), (misfit_hbm, misfit), (tiles_hbm, tiles), (signs_hbm, signs))
        )
    ]
    for load in loads:
        load.start()

    barrier = pltpu.get_barrier_semaphore()
    for off in range(1, n_cols):
        pl.semaphore_signal(
            barrier, inc=1, device_id={"cols": lax.rem(me_c + off, n_cols)},
            device_id_type=pl.DeviceIdType.MESH,
        )
    for off in range(1, n_rows):
        pl.semaphore_signal(
            barrier, inc=1, device_id={"rows": lax.rem(me_r + off, n_rows)},
            device_id_type=pl.DeviceIdType.MESH,
        )

    def send(buf, axis, me, count, send_sem, recv_sem):
        for off in range(1, count):
            pltpu.make_async_remote_copy(
                src_ref=buf.at[me],
                dst_ref=buf.at[me],
                send_sem=send_sem,
                recv_sem=recv_sem,
                device_id={axis: lax.rem(me + off, count)},
                device_id_type=pl.DeviceIdType.MESH,
            ).start()

    def wait_bytes(buf, count, sem):
        view = buf.at[pl.ds(0, count - 1)]
        pltpu.make_async_copy(view, view, sem).wait()

    sub = lax.broadcasted_iota(jnp.int32, (q, LANES), 0)
    loads[0].wait()
    own_weight = jnp.concatenate(
        [weight[pl.ds(rows_s[0, s] * q, q), :] for s in range(slots)], axis=0
    )
    own_squared = own_weight * own_weight
    own_codes = jnp.concatenate([rows_s[0, s] * q + sub for s in range(slots)], axis=0)
    idbuf[me_c, 0:mrows, :] = own_squared
    idbuf[me_c, mrows : 2 * mrows, :] = own_codes.astype(F32)
    loads[1].wait()
    own_misfit = jnp.concatenate(
        [misfit[pl.ds(rows_s[0, s] * q, q), :] for s in range(slots)], axis=0
    )

    lane = lax.broadcasted_iota(jnp.int32, (1, size), 1)
    live = [lane < kept_s[0, s] for s in range(slots)]
    hits = [[cols_s[0, s] == b for b in range(blocks)] for s in range(slots)]
    scale = scale_ref[...]
    depth = to_rows(depth_ref[...], size)
    density = to_rows(density_ref[...], size)

    def adjoint_blocks(field):
        sums = [jnp.zeros((1, size), F32) for _ in range(blocks)]
        for s, row in enumerate(to_rows(field, size)):
            product = nn(row.astype(BF16), tiles[s])
            product = jnp.where(live[s], product, 0.0) * scale
            for b in range(blocks):
                sums[b] = sums[b] + jnp.where(hits[s][b], product, 0.0)
        return sums

    def forward_parts(cells):
        coeffs = haar_apply(nt, [depth[b] * cells[b] for b in range(blocks)], signs[...])
        coeffs = [c * scale for c in coeffs]
        products = []
        for s in range(slots):
            picked = jnp.zeros((1, size), F32)
            for b in range(blocks):
                picked = picked + jnp.where(hits[s][b], coeffs[b], 0.0)
            picked = jnp.where(live[s], picked, 0.0).astype(BF16)
            products.append(nt(picked, tiles[s]))
        return to_lanes(products)

    def put_rows(k, sums):
        for b in range(blocks):
            rowbuf[k, me_r, b : b + 1, :] = sums[b]

    def get_rows(k):
        sums = []
        for b in range(blocks):
            acc = rowbuf[k, 0, b : b + 1, :]
            for r in range(1, n_rows):
                acc = acc + rowbuf[k, r, b : b + 1, :]
            sums.append(acc)
        back = haar_apply(nn, sums, signs[...])
        return [depth[b] * back[b] for b in range(blocks)]

    loads[2].wait()
    put_rows(0, adjoint_blocks((own_squared * own_misfit).astype(BF16).astype(F32)))
    rowbuf[0, me_r, blocks : blocks + 1, :] = jnp.zeros((1, size), F32)
    pl.semaphore_wait(barrier, n_cols + n_rows - 2)
    send(rowbuf.at[0], "rows", me_r, n_rows, row_send.at[0], row_recv.at[0])
    send(idbuf, "cols", me_c, n_cols, id_send.at[0], id_recv.at[0])
    loads[3].wait()

    wait_bytes(rowbuf.at[0], n_rows, row_recv.at[0])
    adj = get_rows(0)
    residual = [adj[b] - DAMPING * density[b] for b in range(blocks)]
    direction = None
    solved = None
    norm_prev = dd = None
    parts_dir = image = change = None
    squared = codes = None

    for k in range(ITERS):
        rr_part = total([residual[b] * residual[b] for b in range(blocks)])
        colbuf[k, me_c, mrows : mrows + 1, :] = jnp.broadcast_to(rr_part, (1, LANES))
        if k:
            rd_part = total([residual[b] * direction[b] for b in range(blocks)])
            colbuf[k, me_c, mrows + 1 : mrows + 2, :] = jnp.broadcast_to(rd_part, (1, LANES))
        else:
            colbuf[k, me_c, mrows + 1 : mrows + 2, :] = jnp.zeros((1, LANES), F32)
        colbuf[k, me_c, 0:mrows, :] = forward_parts(residual)
        send(colbuf.at[k], "cols", me_c, n_cols, col_send.at[k], col_recv.at[k])
        if k == 0:
            wait_bytes(idbuf, n_cols, id_recv.at[0])
            codes = idbuf[:, mrows : 2 * mrows, :].reshape(n, LANES)
            squared = idbuf[:, 0:mrows, :].reshape(n, LANES)
            codes_row = jnp.transpose(codes)[0:1, :]
            match_ref[...] = (codes[:, 0:1] == codes_row).astype(F32).astype(BF16)
        wait_bytes(colbuf.at[k], n_cols, col_recv.at[k])
        parts = colbuf[k, :, 0:mrows, :].reshape(n, LANES)
        norm = colbuf[k, 0, mrows : mrows + 1, :]
        cross = colbuf[k, 0, mrows + 1 : mrows + 2, :]
        for c in range(1, n_cols):
            norm = norm + colbuf[k, c, mrows : mrows + 1, :]
            cross = cross + colbuf[k, c, mrows + 1 : mrows + 2, :]
        new_image = select_dot(match_ref[...], parts)
        if k == 0:
            parts_dir, image = parts, new_image
            direction = residual
            dd = norm
        else:
            beta = norm / norm_prev
            beta_row = jnp.concatenate([beta] * q, axis=1)
            parts_dir = parts + beta * parts_dir
            image = new_image + beta * image
            direction = [residual[b] + beta_row * direction[b] for b in range(blocks)]
            dd = norm + 2.0 * beta * cross + beta * beta * dd
        norm_prev = norm
        curv_part = jnp.sum(
            jnp.sum(parts_dir * (squared * image), axis=0, keepdims=True), axis=1, keepdims=True
        )
        if k + 1 < ITERS:
            image_ref[...] = image
            own_image = image_ref[pl.ds(pl.multiple_of(me_c * mrows, mrows), mrows), :]
            put_rows(k + 1, adjoint_blocks(own_squared * own_image))
            rowbuf[k + 1, me_r, blocks : blocks + 1, :] = jnp.broadcast_to(curv_part, (1, size))
            send(rowbuf.at[k + 1], "rows", me_r, n_rows, row_send.at[k + 1], row_recv.at[k + 1])
            wait_bytes(rowbuf.at[k + 1], n_rows, row_recv.at[k + 1])
            curv = rowbuf[k + 1, 0, blocks : blocks + 1, 0:LANES]
            for r in range(1, n_rows):
                curv = curv + rowbuf[k + 1, r, blocks : blocks + 1, 0:LANES]
        else:
            curvbuf[me_r, :, :] = jnp.broadcast_to(curv_part, (8, LANES))
            send(curvbuf, "rows", me_r, n_rows, curv_send.at[0], curv_recv.at[0])
            wait_bytes(curvbuf, n_rows, curv_recv.at[0])
            curv = curvbuf[0, 0:1, :]
            for r in range(1, n_rows):
                curv = curv + curvbuf[r, 0:1, :]
        alpha = norm / (curv + DAMPING * dd)
        alpha_row = jnp.concatenate([alpha] * q, axis=1)
        if k == 0:
            solved = [alpha_row * direction[b] for b in range(blocks)]
            change = alpha * parts_dir
        else:
            solved = [solved[b] + alpha_row * direction[b] for b in range(blocks)]
            change = change + alpha * parts_dir
        if k + 1 < ITERS:
            adj = get_rows(k + 1)
            residual = [
                residual[b] - alpha_row * (adj[b] + DAMPING * direction[b]) for b in range(blocks)
            ]

    density_out[...] = to_lanes([density[b] + depth[b] * solved[b] for b in range(blocks)])
    share = misfit_out.shape[0]
    wanted = (lax.broadcasted_iota(jnp.int32, (share, n), 0) + me_c * share).astype(F32)
    pick = (wanted == jnp.transpose(codes)[0:1, :]).astype(F32).astype(BF16)
    own_share = misfit[pl.ds(pl.multiple_of(me_c * share, 8), share), :]
    misfit_out[...] = own_share - select_dot(pick, change)

    wait_bytes(idbuf, n_cols, id_send.at[0])
    wait_bytes(curvbuf, n_rows, curv_send.at[0])
    for k in range(ITERS):
        wait_bytes(colbuf.at[k], n_cols, col_send.at[k])
        wait_bytes(rowbuf.at[k], n_rows, row_send.at[k])


def per_device(
    n_rows, n_cols,
    sensitivity, tile_rows, tile_cols, kept_counts, misfit, data_weight, depth_weight, density
):
    slots, size = sensitivity.shape[1], sensitivity.shape[-1]
    q = size // LANES
    data_lanes = misfit.shape[0] // LANES
    cell_lanes = density.shape[0] // LANES
    blocks = density.shape[0] // size
    share = data_lanes // n_cols
    mrows = slots * q
    n = n_cols * mrows
    signs, scale = haar_signs(size)
    vmem = pl.BlockSpec(memory_space=pltpu.VMEM)
    smem = pl.BlockSpec(memory_space=pltpu.SMEM)
    anyspace = pl.BlockSpec(memory_space=pl.ANY)
    dma = pltpu.SemaphoreType.DMA
    new_density, new_misfit = pl.pallas_call(
        functools.partial(kernel, n_rows, n_cols, slots),
        out_shape=(
            jax.ShapeDtypeStruct((cell_lanes, LANES), F32),
            jax.ShapeDtypeStruct((share, LANES), F32),
        ),
        in_specs=[smem] * 3 + [vmem] * 3 + [anyspace] * 4,
        out_specs=(vmem, vmem),
        scratch_shapes=[
            pltpu.VMEM((slots, size, size), BF16),
            pltpu.VMEM((size, size), BF16),
            pltpu.VMEM((data_lanes, LANES), F32),
            pltpu.VMEM((data_lanes, LANES), F32),
            pltpu.VMEM((n_cols, 2 * mrows, LANES), F32),
            pltpu.VMEM((ITERS, n_cols, mrows + 8, LANES), F32),
            pltpu.VMEM((ITERS, n_rows, blocks + 2, size), F32),
            pltpu.VMEM((n_rows, 8, LANES), F32),
            pltpu.VMEM((n, LANES), F32),
            pltpu.VMEM((n, n), BF16),
            dma((4,)), dma((1,)), dma((1,)), dma((ITERS,)), dma((ITERS,)),
            dma((ITERS,)), dma((ITERS,)), dma((1,)), dma((1,)),
        ],
        compiler_params=pltpu.CompilerParams(
            collective_id=0, has_side_effects=True, vmem_limit_bytes=48 * 1024 * 1024
        ),
    )(
        tile_rows, tile_cols, kept_counts, jnp.asarray(scale),
        depth_weight.reshape(cell_lanes, LANES), density.reshape(cell_lanes, LANES),
        sensitivity[0], jnp.asarray(signs, BF16),
        misfit.reshape(data_lanes, LANES), data_weight.reshape(data_lanes, LANES),
    )
    return new_density.reshape(-1), new_misfit.reshape(-1)


def solution(mesh):
    return jax.shard_map(
        functools.partial(per_device, mesh.shape["rows"], mesh.shape["cols"]),
        mesh=mesh,
        in_specs=(
            P("rows", "cols", None, None),
            P("rows", "cols"),
            P("rows", "cols"),
            P("rows", "cols"),
            P("rows"),
            P("rows"),
            P("cols"),
            P("cols"),
        ),
        out_specs=(P("cols"), P(("rows", "cols"))),
        check_vma=False,
    )
```

time: 382 us -> 55 us (0.14)
  waiting for transfers between devices: 211 us -> 0 us
  blocking collectives: 108 us -> 0 us
  Pallas kernels: 0 us -> 44.2 us
  matrix products: 22.4 us -> 0 us
  between operations: 22.5 us -> 0.66 us
  other arithmetic: 11.7 us -> 0 us
    psum x4 -> x0, waiting for transfers between devices: 211 us -> none  [per_device(): image_data = lax.psum(partial_data, 'cols')]
    psum x9 -> x0, blocking collectives: 108 us -> none  [the longest x5 50.7 us: adjoint_part(): return lax.psum(cell_part, 'rows')]
    pallas_call x0 -> x1, Pallas kernels: none -> 44.2 us  [per_device(): pl.pallas_call(functools.partial(kernel, n_rows, n_cols, slots), out_shap...]
    dot_general x36 -> x0, matrix products: 22.4 us -> none  [the longest x5 4.98 us: adjoint_part(): jnp.dot(pick_rows.astype(jnp.bfloat16), data_rows, preferred_element_type...]
    unnamed x41 -> x22, local copies, waits for them, and re-layouts: 3.23 us -> 9.75 us
    convert_element_type x5 -> x0, other arithmetic: 5.08 us -> none  [the longest x4 3.9 us: per_device(): weighted = (squared * image_data).astype(jnp.bfloat16)]
  transfers between devices with their start and end apart: 4 -> 0, of which waited for: 4 -> 0; matrix products, arithmetic and copies ran while one was open for 0% -> 0% of each run, Pallas kernels for 0% -> 0%
where the time goes in v1:
time: 55 us; the launch traced here: 54.6 us
  Pallas kernels  44.2 us (80%)
  local copies, waits for them, and re-layouts  9.75 us (18%)
  between operations  0.66 us (1%)
    pallas_call x1, Pallas kernels, per_device(): pl.pallas_call(functools.partial(kernel, n_rows, n_cols, slots), out_shap...  44.2 us
    unnamed x22, local copies, waits for them, and re-layouts  9.75 us

profile of v1, /device:TPU:0, one launch (start us, length us, event | category | flops | bytes accessed | tf_op | source)
XLA Modules:
  0.0 54.6 jit_solution(14998133285988213287)
XLA Ops:
  0.6 0.0 copy-start
  0.6 1.6 %copy-done = bf16[1,4,512,512]{3,2,1,0:T(8,128)(2,1)S(1)} copy-done((bf16[1,4,512,512]{3,2,1,0:T(8,128)(2,1)S(1)}, bf16[1,4,512,512]{3,2,1,0:T(8,128)(2,1)}, u32[]{:S(2)}) %copy-start) | copy-done | bytes 2097176
  2.2 0.0 copy-start.1
  2.2 1.0 %copy-done.1 = bf16[512,512]{1,0:T(8,128)(2,1)S(1)} copy-done((bf16[512,512]{1,0:T(8,128)(2,1)S(1)}, bf16[512,512]{1,0:T(8,128)(2,1)}, u32[]{:S(2)}) %copy-start.1) | copy-done | bytes 524312
  3.3 0.0 copy-start.2
  3.3 0.9 %copy-done.2 = f32[65536]{0:T(1024)S(1)} copy-done((f32[65536]{0:T(1024)S(1)}, f32[65536]{0:T(1024)}, u32[]{:S(2)}) %copy-start.2) | copy-done | bytes 262168
  4.2 0.0 copy-start.3
  4.2 0.9 %copy-done.3 = f32[65536]{0:T(1024)S(1)} copy-done((f32[65536]{0:T(1024)S(1)}, f32[65536]{0:T(1024)}, u32[]{:S(2)}) %copy-start.3) | copy-done | bytes 262168
  5.2 0.0 copy-start.4
  5.2 0.7 %copy-done.4 = f32[1024]{0:T(1024)S(1)} copy-done((f32[1024]{0:T(1024)S(1)}, f32[1024]{0:T(1024)}, u32[]{:S(2)}) %copy-start.4) | copy-done | bytes 4120
  5.9 0.0 copy-start.5
  5.9 0.7 %copy-done.5 = f32[1024]{0:T(1024)S(1)} copy-done((f32[1024]{0:T(1024)S(1)}, f32[1024]{0:T(1024)}, u32[]{:S(2)}) %copy-start.5) | copy-done | bytes 4120
  6.5 0.0 copy-start.6
  6.5 0.7 %copy-done.6 = f32[1,512]{1,0:T(1,128)S(1)} copy-done((f32[1,512]{1,0:T(1,128)S(1)}, f32[1,512]{1,0:T(1,128)}, u32[]{:S(2)}) %copy-start.6) | copy-done | bytes 2072
  7.2 0.0 copy-start.7
  7.2 0.7 %copy-done.7 = s32[1,4]{1,0:T(1,128)S(1)} copy-done((s32[1,4]{1,0:T(1,128)S(1)}, s32[1,4]{1,0:T(1,128)}, u32[]{:S(2)}) %copy-start.7) | copy-done | bytes 40
  7.9 0.0 copy-start.8
  7.9 0.7 %copy-done.8 = s32[1,4]{1,0:T(1,128)S(1)} copy-done((s32[1,4]{1,0:T(1,128)S(1)}, s32[1,4]{1,0:T(1,128)}, u32[]{:S(2)}) %copy-start.8) | copy-done | bytes 40
  8.5 0.0 copy-start.9
  8.5 0.7 %copy-done.9 = s32[1,4]{1,0:T(1,128)S(1)} copy-done((s32[1,4]{1,0:T(1,128)S(1)}, s32[1,4]{1,0:T(1,128)}, u32[]{:S(2)}) %copy-start.9) | copy-done | bytes 40
  9.2 44.2 %shard_map.113 = (f32[8,128]{1,0:T(8,128)S(1)}, f32[64,128]{1,0:T(8,128)S(1)}) custom-call(s32[1,4]{1,0:T(1,128)S(1)} %copy-done.7, s32[1,4]{1,0:T(1,128)S(1)} %copy-done.8, s32[1,4]{1,0:T(1,128)S(1)} %copy-done.9, f32[1,512]{1,0:T(1,128)S(1)} %copy-done.6, f32[8,128]{1,0:T(8,128)S(1)} %bitcast.11, f32[8,128]{1,0:T(8,128)S(1)} %bitcast.12, ...), custom_call_target="tpu_custom_call" | custom-call | tf_op jit(solution)/shard_map/pallas_call | solution.py:312
  53.4 0.6 %copy.14 = f32[1024]{0:T(1024)} copy(f32[1024]{0:T(1024)S(1)} %bitcast.13) | data formatting | bytes 8192
  54.0 0.6 %copy.15 = f32[8192]{0:T(1024)} copy(f32[8192]{0:T(1024)S(1)} %bitcast.10) | data formatting | bytes 65536
Async XLA Ops:
  0.6 1.6 %copy-start = (bf16[1,4,512,512]{3,2,1,0:T(8,128)(2,1)S(1)}, bf16[1,4,512,512]{3,2,1,0:T(8,128)(2,1)}, u32[]{:S(2)}) copy-start(bf16[1,4,512,512]{3,2,1,0:T(8,128)(2,1)} %param.10) | copy-start | bytes 6291460
  2.2 1.0 %copy-start.1 = (bf16[512,512]{1,0:T(8,128)(2,1)S(1)}, bf16[512,512]{1,0:T(8,128)(2,1)}, u32[]{:S(2)}) copy-start(bf16[512,512]{1,0:T(8,128)(2,1)} %constant.5.clone.signs_hbm) | copy-start | bytes 1572868
  3.3 0.9 %copy-start.2 = (f32[65536]{0:T(1024)S(1)}, f32[65536]{0:T(1024)}, u32[]{:S(2)}) copy-start(f32[65536]{0:T(1024)} %param.14) | copy-start | bytes 786436
  4.2 0.9 %copy-start.3 = (f32[65536]{0:T(1024)S(1)}, f32[65536]{0:T(1024)}, u32[]{:S(2)}) copy-start(f32[65536]{0:T(1024)} %param.15) | copy-start | bytes 786436
  5.2 0.7 %copy-start.4 = (f32[1024]{0:T(1024)S(1)}, f32[1024]{0:T(1024)}, u32[]{:S(2)}) copy-start(f32[1024]{0:T(1024)} %param.16) | copy-start | bytes 12292
  5.9 0.7 %copy-start.5 = (f32[1024]{0:T(1024)S(1)}, f32[1024]{0:T(1024)}, u32[]{:S(2)}) copy-start(f32[1024]{0:T(1024)} %param.17) | copy-start | bytes 12292
  6.5 0.7 %copy-start.6 = (f32[1,512]{1,0:T(1,128)S(1)}, f32[1,512]{1,0:T(1,128)}, u32[]{:S(2)}) copy-start(f32[1,512]{1,0:T(1,128)} %constant.4.clone.scale_ref) | copy-start | bytes 6148
  7.2 0.7 %copy-start.7 = (s32[1,4]{1,0:T(1,128)S(1)}, s32[1,4]{1,0:T(1,128)}, u32[]{:S(2)}) copy-start(s32[1,4]{1,0:T(1,128)} %rows_s.1) | copy-start | bytes 52
  7.9 0.7 %copy-start.8 = (s32[1,4]{1,0:T(1,128)S(1)}, s32[1,4]{1,0:T(1,128)}, u32[]{:S(2)}) copy-start(s32[1,4]{1,0:T(1,128)} %cols_s.1) | copy-start | bytes 52
  8.5 0.7 %copy-start.9 = (s32[1,4]{1,0:T(1,128)S(1)}, s32[1,4]{1,0:T(1,128)}, u32[]{:S(2)}) copy-start(s32[1,4]{1,0:T(1,128)} %kept_s.1) | copy-start | bytes 52

commit v2 on v1

--- a/solution.py
+++ b/solution.py
@@ -84,9 +84,10 @@
 
 def kernel(
     n_rows, n_cols, slots,
-    rows_s, cols_s, kept_s, scale_ref, depth_ref, density_ref,
+    rows_hbm, cols_hbm, kept_hbm, scale_hbm, depth_hbm, density_hbm,
     tiles_hbm, signs_hbm, misfit_hbm, weight_hbm,
     density_out, misfit_out,
+    rows_s, cols_s, kept_s, scale_ref, depth_ref, density_ref,
     tiles, signs, misfit, weight,
     idbuf, colbuf, rowbuf, curvbuf, image_ref, match_ref,
     load_sem, id_send, id_recv, col_send, col_recv, row_send, row_recv, curv_send, curv_recv,
@@ -102,7 +103,12 @@
     loads = [
         pltpu.make_async_copy(src, dst, load_sem.at[i])
         for i, (src, dst) in enumerate(
-            ((weight_hbm, weight), (misfit_hbm, misfit), (tiles_hbm, tiles), (signs_hbm, signs))
+            (
+                (rows_hbm, rows_s), (weight_hbm, weight), (misfit_hbm, misfit),
+                (kept_hbm, kept_s), (cols_hbm, cols_s), (scale_hbm, scale_ref),
+                (tiles_hbm, tiles), (signs_hbm, signs),
+                (depth_hbm, depth_ref), (density_hbm, density_ref),
+            )
         )
     ]
     for load in loads:
@@ -137,6 +143,7 @@
 
     sub = lax.broadcasted_iota(jnp.int32, (q, LANES), 0)
     loads[0].wait()
+    loads[1].wait()
     own_weight = jnp.concatenate(
         [weight[pl.ds(rows_s[0, s] * q, q), :] for s in range(slots)], axis=0
     )
@@ -144,17 +151,17 @@
     own_codes = jnp.concatenate([rows_s[0, s] * q + sub for s in range(slots)], axis=0)
     idbuf[me_c, 0:mrows, :] = own_squared
     idbuf[me_c, mrows : 2 * mrows, :] = own_codes.astype(F32)
-    loads[1].wait()
+    loads[2].wait()
     own_misfit = jnp.concatenate(
         [misfit[pl.ds(rows_s[0, s] * q, q), :] for s in range(slots)], axis=0
     )
 
+    for i in (3, 4, 5):
+        loads[i].wait()
     lane = lax.broadcasted_iota(jnp.int32, (1, size), 1)
     live = [lane < kept_s[0, s] for s in range(slots)]
     hits = [[cols_s[0, s] == b for b in range(blocks)] for s in range(slots)]
     scale = scale_ref[...]
-    depth = to_rows(depth_ref[...], size)
-    density = to_rows(density_ref[...], size)
 
     def adjoint_blocks(field):
         sums = [jnp.zeros((1, size), F32) for _ in range(blocks)]
@@ -191,13 +198,16 @@
         back = haar_apply(nn, sums, signs[...])
         return [depth[b] * back[b] for b in range(blocks)]
 
-    loads[2].wait()
+    loads[6].wait()
     put_rows(0, adjoint_blocks((own_squared * own_misfit).astype(BF16).astype(F32)))
     rowbuf[0, me_r, blocks : blocks + 1, :] = jnp.zeros((1, size), F32)
     pl.semaphore_wait(barrier, n_cols + n_rows - 2)
     send(rowbuf.at[0], "rows", me_r, n_rows, row_send.at[0], row_recv.at[0])
     send(idbuf, "cols", me_c, n_cols, id_send.at[0], id_recv.at[0])
-    loads[3].wait()
+    for i in (7, 8, 9):
+        loads[i].wait()
+    depth = to_rows(depth_ref[...], size)
+    density = to_rows(density_ref[...], size)
 
     wait_bytes(rowbuf.at[0], n_rows, row_recv.at[0])
     adj = get_rows(0)
@@ -306,8 +316,7 @@
     n = n_cols * mrows
     signs, scale = haar_signs(size)
     vmem = pl.BlockSpec(memory_space=pltpu.VMEM)
-    smem = pl.BlockSpec(memory_space=pltpu.SMEM)
-    anyspace = pl.BlockSpec(memory_space=pl.ANY)
+    hbm = pl.BlockSpec(memory_space=pltpu.HBM)
     dma = pltpu.SemaphoreType.DMA
     new_density, new_misfit = pl.pallas_call(
         functools.partial(kernel, n_rows, n_cols, slots),
@@ -315,9 +324,15 @@
             jax.ShapeDtypeStruct((cell_lanes, LANES), F32),
             jax.ShapeDtypeStruct((share, LANES), F32),
         ),
-        in_specs=[smem] * 3 + [vmem] * 3 + [anyspace] * 4,
+        in_specs=[hbm] * 10,
         out_specs=(vmem, vmem),
         scratch_shapes=[
+            pltpu.SMEM((1, slots), jnp.int32),
+            pltpu.SMEM((1, slots), jnp.int32),
+            pltpu.SMEM((1, slots), jnp.int32),
+            pltpu.VMEM((1, size), F32),
+            pltpu.VMEM((cell_lanes, LANES), F32),
+            pltpu.VMEM((cell_lanes, LANES), F32),
             pltpu.VMEM((slots, size, size), BF16),
             pltpu.VMEM((size, size), BF16),
             pltpu.VMEM((data_lanes, LANES), F32),
@@ -328,11 +343,11 @@
             pltpu.VMEM((n_rows, 8, LANES), F32),
             pltpu.VMEM((n, LANES), F32),
             pltpu.VMEM((n, n), BF16),
-            dma((4,)), dma((1,)), dma((1,)), dma((ITERS,)), dma((ITERS,)),
+            dma((10,)), dma((1,)), dma((1,)), dma((ITERS,)), dma((ITERS,)),
             dma((ITERS,)), dma((ITERS,)), dma((1,)), dma((1,)),
         ],
         compiler_params=pltpu.CompilerParams(
-            collective_id=0, has_side_effects=True, vmem_limit_bytes=48 * 1024 * 1024
+            collective_id=0, has_side_effects=True, vmem_limit_bytes=67_043_328
         ),
     )(
         tile_rows, tile_cols, kept_counts, jnp.asarray(scale),

time: 55 us -> 47.6 us (0.87)
  local copies, waits for them, and re-layouts: 9.75 us -> 2.65 us
    unnamed x22 -> x2, local copies, waits for them, and re-layouts: 9.75 us -> 2.65 us
where the time goes in v2:
time: 47.6 us; the launch traced here: 47.4 us
  Pallas kernels  44.1 us (93%)
  local copies, waits for them, and re-layouts  2.65 us (6%)
  between operations  0.64 us (1%)
    pallas_call x1, Pallas kernels, per_device(): pl.pallas_call(functools.partial(kernel, n_rows, n_cols, slots), out_shap...  44.1 us
    unnamed x2, local copies, waits for them, and re-layouts  2.65 us

profile of v2, /device:TPU:0, one launch (start us, length us, event | category | flops | bytes accessed | tf_op | source)
XLA Modules:
  0.0 47.4 jit_solution(11880459244497127322)
XLA Ops:
  0.6 44.1 %shard_map.113 = (f32[8,128]{1,0:T(8,128)}, f32[64,128]{1,0:T(8,128)}) custom-call(s32[1,4]{1,0:T(1,128)} %rows_hbm.1, s32[1,4]{1,0:T(1,128)} %cols_hbm.1, s32[1,4]{1,0:T(1,128)} %kept_hbm.1, f32[1,512]{1,0:T(1,128)} %constant.4.clone.scale_hbm, f32[8,128]{1,0:T(8,128)} %bitcast.11, f32[8,128]{1,0:T(8,128)} %bitcast.12, bf16[4,512,512]{2,1,0:T(8,128)(2,1)} %bitcast.7, ...), custom_call_target="tpu_custom_call" | custom-call | tf_op jit(solution)/shard_map/pallas_call | solution.py:321
  44.8 1.3 %copy.14 = f32[1024]{0:T(1024)} copy(f32[1024]{0:T(1024)} %bitcast.13) | data formatting | bytes 8192
  46.0 1.4 %copy.15 = f32[8192]{0:T(1024)} copy(f32[8192]{0:T(1024)} %bitcast.10) | data formatting | bytes 65536

commit v3 on v2

--- a/solution.py
+++ b/solution.py
@@ -89,8 +89,9 @@
     density_out, misfit_out,
     rows_s, cols_s, kept_s, scale_ref, depth_ref, density_ref,
     tiles, signs, misfit, weight,
-    idbuf, colbuf, rowbuf, curvbuf, image_ref, match_ref,
-    load_sem, id_send, id_recv, col_send, col_recv, row_send, row_recv, curv_send, curv_recv,
+    idbuf, colbuf, dotbuf, rowbuf, curvbuf, image_ref, match_ref,
+    load_sem, id_send, id_recv, col_send, col_recv, dot_send, dot_recv,
+    row_send, row_recv, curv_send, curv_recv,
 ):
     size = tiles.shape[-1]
     q = size // LANES
@@ -126,14 +127,22 @@
             device_id_type=pl.DeviceIdType.MESH,
         )
 
+    def far_first(me, count):
+        upper = (2 * me) // count
+        for j in range(count - 1):
+            down = count - 1 - j
+            down = down - lax.select(down <= me, 1, 0)
+            up = j + lax.select(j >= me, 1, 0)
+            yield down + upper * (up - down)
+
     def send(buf, axis, me, count, send_sem, recv_sem):
-        for off in range(1, count):
+        for peer in far_first(me, count):
             pltpu.make_async_remote_copy(
                 src_ref=buf.at[me],
                 dst_ref=buf.at[me],
                 send_sem=send_sem,
                 recv_sem=recv_sem,
-                device_id={axis: lax.rem(me + off, count)},
+                device_id={axis: peer},
                 device_id_type=pl.DeviceIdType.MESH,
             ).start()
 
@@ -200,7 +209,6 @@
 
     loads[6].wait()
     put_rows(0, adjoint_blocks((own_squared * own_misfit).astype(BF16).astype(F32)))
-    rowbuf[0, me_r, blocks : blocks + 1, :] = jnp.zeros((1, size), F32)
     pl.semaphore_wait(barrier, n_cols + n_rows - 2)
     send(rowbuf.at[0], "rows", me_r, n_rows, row_send.at[0], row_recv.at[0])
     send(idbuf, "cols", me_c, n_cols, id_send.at[0], id_recv.at[0])
@@ -219,14 +227,15 @@
     squared = codes = None
 
     for k in range(ITERS):
-        rr_part = total([residual[b] * residual[b] for b in range(blocks)])
-        colbuf[k, me_c, mrows : mrows + 1, :] = jnp.broadcast_to(rr_part, (1, LANES))
+        dots = [total([residual[b] * residual[b] for b in range(blocks)])]
         if k:
-            rd_part = total([residual[b] * direction[b] for b in range(blocks)])
-            colbuf[k, me_c, mrows + 1 : mrows + 2, :] = jnp.broadcast_to(rd_part, (1, LANES))
+            dots.append(total([residual[b] * direction[b] for b in range(blocks)]))
         else:
-            colbuf[k, me_c, mrows + 1 : mrows + 2, :] = jnp.zeros((1, LANES), F32)
-        colbuf[k, me_c, 0:mrows, :] = forward_parts(residual)
+            dots.append(jnp.zeros((1, 1), F32))
+        for i in range(2):
+            dotbuf[k, me_c, i : i + 1, :] = jnp.broadcast_to(dots[i], (1, LANES))
+        send(dotbuf.at[k], "cols", me_c, n_cols, dot_send.at[k], dot_recv.at[k])
+        colbuf[k, me_c, :, :] = forward_parts(residual).astype(BF16)
         send(colbuf.at[k], "cols", me_c, n_cols, col_send.at[k], col_recv.at[k])
         if k == 0:
             wait_bytes(idbuf, n_cols, id_recv.at[0])
@@ -234,14 +243,16 @@
             squared = idbuf[:, 0:mrows, :].reshape(n, LANES)
             codes_row = jnp.transpose(codes)[0:1, :]
             match_ref[...] = (codes[:, 0:1] == codes_row).astype(F32).astype(BF16)
+        wait_bytes(dotbuf.at[k], n_cols, dot_recv.at[k])
+        norm = dotbuf[k, 0, 0:1, :]
+        cross = dotbuf[k, 0, 1:2, :]
+        for c in range(1, n_cols):
+            norm = norm + dotbuf[k, c, 0:1, :]
+            cross = cross + dotbuf[k, c, 1:2, :]
         wait_bytes(colbuf.at[k], n_cols, col_recv.at[k])
-        parts = colbuf[k, :, 0:mrows, :].reshape(n, LANES)
-        norm = colbuf[k, 0, mrows : mrows + 1, :]
-        cross = colbuf[k, 0, mrows + 1 : mrows + 2, :]
-        for c in range(1, n_cols):
-            norm = norm + colbuf[k, c, mrows : mrows + 1, :]
-            cross = cross + colbuf[k, c, mrows + 1 : mrows + 2, :]
-        new_image = select_dot(match_ref[...], parts)
+        parts = colbuf[k].reshape(n, LANES)
+        new_image = nn(match_ref[...], parts)
+        parts = parts.astype(F32)
         if k == 0:
             parts_dir, image = parts, new_image
             direction = residual
@@ -261,19 +272,16 @@
             image_ref[...] = image
             own_image = image_ref[pl.ds(pl.multiple_of(me_c * mrows, mrows), mrows), :]
             put_rows(k + 1, adjoint_blocks(own_squared * own_image))
-            rowbuf[k + 1, me_r, blocks : blocks + 1, :] = jnp.broadcast_to(curv_part, (1, size))
             send(rowbuf.at[k + 1], "rows", me_r, n_rows, row_send.at[k + 1], row_recv.at[k + 1])
+        curvbuf[k, me_r, :, :] = jnp.broadcast_to(curv_part, (1, LANES))
+        send(curvbuf.at[k], "rows", me_r, n_rows, curv_send.at[k], curv_recv.at[k])
+        if k + 1 < ITERS:
             wait_bytes(rowbuf.at[k + 1], n_rows, row_recv.at[k + 1])
-            curv = rowbuf[k + 1, 0, blocks : blocks + 1, 0:LANES]
-            for r in range(1, n_rows):
-                curv = curv + rowbuf[k + 1, r, blocks : blocks + 1, 0:LANES]
-        else:
-            curvbuf[me_r, :, :] = jnp.broadcast_to(curv_part, (8, LANES))
-            send(curvbuf, "rows", me_r, n_rows, curv_send.at[0], curv_recv.at[0])
-            wait_bytes(curvbuf, n_rows, curv_recv.at[0])
-            curv = curvbuf[0, 0:1, :]
-            for r in range(1, n_rows):
-                curv = curv + curvbuf[r, 0:1, :]
+            adj = get_rows(k + 1)
+        wait_bytes(curvbuf.at[k], n_rows, curv_recv.at[k])
+        curv = curvbuf[k, 0, 0:1, :]
+        for r in range(1, n_rows):
+            curv = curv + curvbuf[k, r, 0:1, :]
         alpha = norm / (curv + DAMPING * dd)
         alpha_row = jnp.concatenate([alpha] * q, axis=1)
         if k == 0:
@@ -283,7 +291,6 @@
             solved = [solved[b] + alpha_row * direction[b] for b in range(blocks)]
             change = change + alpha * parts_dir
         if k + 1 < ITERS:
-            adj = get_rows(k + 1)
             residual = [
                 residual[b] - alpha_row * (adj[b] + DAMPING * direction[b]) for b in range(blocks)
             ]
@@ -296,10 +303,11 @@
     misfit_out[...] = own_share - select_dot(pick, change)
 
     wait_bytes(idbuf, n_cols, id_send.at[0])
-    wait_bytes(curvbuf, n_rows, curv_send.at[0])
     for k in range(ITERS):
         wait_bytes(colbuf.at[k], n_cols, col_send.at[k])
+        wait_bytes(dotbuf.at[k], n_cols, dot_send.at[k])
         wait_bytes(rowbuf.at[k], n_rows, row_send.at[k])
+        wait_bytes(curvbuf.at[k], n_rows, curv_send.at[k])
 
 
 def per_device(
@@ -338,13 +346,14 @@
             pltpu.VMEM((data_lanes, LANES), F32),
             pltpu.VMEM((data_lanes, LANES), F32),
             pltpu.VMEM((n_cols, 2 * mrows, LANES), F32),
-            pltpu.VMEM((ITERS, n_cols, mrows + 8, LANES), F32),
-            pltpu.VMEM((ITERS, n_rows, blocks + 2, size), F32),
-            pltpu.VMEM((n_rows, 8, LANES), F32),
+            pltpu.VMEM((ITERS, n_cols, mrows, LANES), BF16),
+            pltpu.VMEM((ITERS, n_cols, 2, LANES), F32),
+            pltpu.VMEM((ITERS, n_rows, blocks, size), F32),
+            pltpu.VMEM((ITERS, n_rows, 1, LANES), F32),
             pltpu.VMEM((n, LANES), F32),
             pltpu.VMEM((n, n), BF16),
             dma((10,)), dma((1,)), dma((1,)), dma((ITERS,)), dma((ITERS,)),
-            dma((ITERS,)), dma((ITERS,)), dma((1,)), dma((1,)),
+            dma((ITERS,)), dma((ITERS,)), dma((ITERS,)), dma((ITERS,)), dma((ITERS,)), dma((ITERS,)),
         ],
         compiler_params=pltpu.CompilerParams(
             collective_id=0, has_side_effects=True, vmem_limit_bytes=67_043_328

time: 47.6 us -> 46.5 us (0.977)
  Pallas kernels: 44.1 us -> 43 us
    pallas_call x1, Pallas kernels: 44.1 us -> 43 us  [per_device(): pl.pallas_call(functools.partial(kernel, n_rows, n_cols, slots), out_shap...]
where the time goes in v3:
time: 46.5 us; the launch traced here: 46.3 us
  Pallas kernels  43 us (92%)
  local copies, waits for them, and re-layouts  2.65 us (6%)
  between operations  0.64 us (1%)
    pallas_call x1, Pallas kernels, per_device(): pl.pallas_call(functools.partial(kernel, n_rows, n_cols, slots), out_shap...  43 us
    unnamed x2, local copies, waits for them, and re-layouts  2.65 us

profile of v3, /device:TPU:0, one launch (start us, length us, event | category | flops | bytes accessed | tf_op | source)
XLA Modules:
  0.0 46.3 jit_solution(6167175117189515230)
XLA Ops:
  0.6 43.0 %shard_map.113 = (f32[8,128]{1,0:T(8,128)}, f32[64,128]{1,0:T(8,128)}) custom-call(s32[1,4]{1,0:T(1,128)} %rows_hbm.1, s32[1,4]{1,0:T(1,128)} %cols_hbm.1, s32[1,4]{1,0:T(1,128)} %kept_hbm.1, f32[1,512]{1,0:T(1,128)} %constant.4.clone.scale_hbm, f32[8,128]{1,0:T(8,128)} %bitcast.11, f32[8,128]{1,0:T(8,128)} %bitcast.12, bf16[4,512,512]{2,1,0:T(8,128)(2,1)} %bitcast.7, ...), custom_call_target="tpu_custom_call" | custom-call | tf_op jit(solution)/shard_map/pallas_call | solution.py:329
  43.6 1.3 %copy.14 = f32[1024]{0:T(1024)} copy(f32[1024]{0:T(1024)} %bitcast.13) | data formatting | bytes 8192
  44.9 1.4 %copy.15 = f32[8192]{0:T(1024)} copy(f32[8192]{0:T(1024)} %bitcast.10) | data formatting | bytes 65536

commit v4 on v3

--- a/solution.py
+++ b/solution.py
@@ -16,19 +16,19 @@
 BF16 = jnp.bfloat16
 
 
-def haar_signs(size):
-    signs = np.zeros((size, size), np.float32)
-    scale = np.zeros((1, size), np.float32)
-    signs[0] = 1.0
-    scale[0, 0] = 1.0 / math.sqrt(size)
+def haar_matrix(size):
+    matrix = np.zeros((size, size), np.float32)
+    matrix[0] = 1.0 / math.sqrt(size)
     for n in range(1, size):
         level = n.bit_length() - 1
         k = n - (1 << level)
         support = size >> level
-        signs[n, k * support : k * support + support // 2] = 1.0
-        signs[n, k * support + support // 2 : (k + 1) * support] = -1.0
-        scale[0, n] = 1.0 / math.sqrt(support)
-    return signs, scale
+        value = 1.0 / math.sqrt(support)
+        matrix[n, k * support : k * support + support // 2] = value
+        matrix[n, k * support + support // 2 : (k + 1) * support] = -value
+    high = matrix.astype(BF16)
+    low = (matrix - high.astype(np.float32)).astype(BF16)
+    return high, low
 
 
 def split3(x):
@@ -67,14 +67,6 @@
     )
 
 
-def haar_apply(dot, rows, matrix):
-    m = len(rows)
-    parts = [split3(row) for row in rows]
-    lhs = jnp.concatenate([p[t].astype(F32) for t in range(3) for p in parts], axis=0).astype(BF16)
-    out = dot(lhs, matrix)
-    return [out[i : i + 1] + (out[m + i : m + i + 1] + out[2 * m + i : 2 * m + i + 1]) for i in range(m)]
-
-
 def total(rows):
     acc = rows[0]
     for row in rows[1:]:
@@ -84,11 +76,11 @@
 
 def kernel(
     n_rows, n_cols, slots,
-    rows_hbm, cols_hbm, kept_hbm, scale_hbm, depth_hbm, density_hbm,
-    tiles_hbm, signs_hbm, misfit_hbm, weight_hbm,
+    rows_hbm, cols_hbm, kept_hbm, depth_hbm, density_hbm,
+    tiles_hbm, high_hbm, low_hbm, misfit_hbm, weight_hbm,
     density_out, misfit_out,
-    rows_s, cols_s, kept_s, scale_ref, depth_ref, density_ref,
-    tiles, signs, misfit, weight,
+    rows_s, cols_s, kept_s, depth_ref, density_ref,
+    tiles, high, low, misfit, weight,
     idbuf, colbuf, dotbuf, rowbuf, curvbuf, image_ref, match_ref,
     load_sem, id_send, id_recv, col_send, col_recv, dot_send, dot_recv,
     row_send, row_recv, curv_send, curv_recv,
@@ -105,10 +97,9 @@
         pltpu.make_async_copy(src, dst, load_sem.at[i])
         for i, (src, dst) in enumerate(
             (
-                (rows_hbm, rows_s), (weight_hbm, weight), (misfit_hbm, misfit),
-                (kept_hbm, kept_s), (cols_hbm, cols_s), (scale_hbm, scale_ref),
-                (tiles_hbm, tiles), (signs_hbm, signs),
-                (depth_hbm, depth_ref), (density_hbm, density_ref),
+                (kept_hbm, kept_s), (cols_hbm, cols_s), (rows_hbm, rows_s), (depth_hbm, depth_ref),
+                (tiles_hbm, tiles), (high_hbm, high), (low_hbm, low),
+                (weight_hbm, weight), (misfit_hbm, misfit), (density_hbm, density_ref),
             )
         )
     ]
@@ -150,9 +141,9 @@
         view = buf.at[pl.ds(0, count - 1)]
         pltpu.make_async_copy(view, view, sem).wait()
 
+    for load in loads:
+        load.wait()
     sub = lax.broadcasted_iota(jnp.int32, (q, LANES), 0)
-    loads[0].wait()
-    loads[1].wait()
     own_weight = jnp.concatenate(
         [weight[pl.ds(rows_s[0, s] * q, q), :] for s in range(slots)], axis=0
     )
@@ -160,37 +151,38 @@
     own_codes = jnp.concatenate([rows_s[0, s] * q + sub for s in range(slots)], axis=0)
     idbuf[me_c, 0:mrows, :] = own_squared
     idbuf[me_c, mrows : 2 * mrows, :] = own_codes.astype(F32)
-    loads[2].wait()
     own_misfit = jnp.concatenate(
         [misfit[pl.ds(rows_s[0, s] * q, q), :] for s in range(slots)], axis=0
     )
 
-    for i in (3, 4, 5):
-        loads[i].wait()
     lane = lax.broadcasted_iota(jnp.int32, (1, size), 1)
-    live = [lane < kept_s[0, s] for s in range(slots)]
     hits = [[cols_s[0, s] == b for b in range(blocks)] for s in range(slots)]
-    scale = scale_ref[...]
+    depth = to_rows(depth_ref[...], size)
+    density = to_rows(density_ref[...], size)
+
+    for s in range(slots):
+        live = jnp.where(lane < kept_s[0, s], 1.0, 0.0).astype(BF16)
+        masked = tiles[s] * live
+        cell_weight = jnp.zeros((1, size), F32)
+        for b in range(blocks):
+            cell_weight = cell_weight + jnp.where(hits[s][b], depth[b], 0.0)
+        tiles[s] = ((nn(masked, high[...]) + nn(masked, low[...])) * cell_weight).astype(BF16)
 
     def adjoint_blocks(field):
         sums = [jnp.zeros((1, size), F32) for _ in range(blocks)]
         for s, row in enumerate(to_rows(field, size)):
             product = nn(row.astype(BF16), tiles[s])
-            product = jnp.where(live[s], product, 0.0) * scale
             for b in range(blocks):
                 sums[b] = sums[b] + jnp.where(hits[s][b], product, 0.0)
         return sums
 
     def forward_parts(cells):
-        coeffs = haar_apply(nt, [depth[b] * cells[b] for b in range(blocks)], signs[...])
-        coeffs = [c * scale for c in coeffs]
         products = []
         for s in range(slots):
             picked = jnp.zeros((1, size), F32)
             for b in range(blocks):
-                picked = picked + jnp.where(hits[s][b], coeffs[b], 0.0)
-            picked = jnp.where(live[s], picked, 0.0).astype(BF16)
-            products.append(nt(picked, tiles[s]))
+                picked = picked + jnp.where(hits[s][b], cells[b], 0.0)
+            products.append(nt(picked.astype(BF16), tiles[s]))
         return to_lanes(products)
 
     def put_rows(k, sums):
@@ -204,19 +196,12 @@
             for r in range(1, n_rows):
                 acc = acc + rowbuf[k, r, b : b + 1, :]
             sums.append(acc)
-        back = haar_apply(nn, sums, signs[...])
-        return [depth[b] * back[b] for b in range(blocks)]
-
-    loads[6].wait()
+        return sums
+
     put_rows(0, adjoint_blocks((own_squared * own_misfit).astype(BF16).astype(F32)))
     pl.semaphore_wait(barrier, n_cols + n_rows - 2)
     send(rowbuf.at[0], "rows", me_r, n_rows, row_send.at[0], row_recv.at[0])
     send(idbuf, "cols", me_c, n_cols, id_send.at[0], id_recv.at[0])
-    for i in (7, 8, 9):
-        loads[i].wait()
-    depth = to_rows(depth_ref[...], size)
-    density = to_rows(density_ref[...], size)
-
     wait_bytes(rowbuf.at[0], n_rows, row_recv.at[0])
     adj = get_rows(0)
     residual = [adj[b] - DAMPING * density[b] for b in range(blocks)]
@@ -275,6 +260,13 @@
             send(rowbuf.at[k + 1], "rows", me_r, n_rows, row_send.at[k + 1], row_recv.at[k + 1])
         curvbuf[k, me_r, :, :] = jnp.broadcast_to(curv_part, (1, LANES))
         send(curvbuf.at[k], "rows", me_r, n_rows, curv_send.at[k], curv_recv.at[k])
+        if k + 1 == ITERS:
+            share = misfit_out.shape[0]
+            wanted = (lax.broadcasted_iota(jnp.int32, (share, n), 0) + me_c * share).astype(F32)
+            pick = (wanted == jnp.transpose(codes)[0:1, :]).astype(F32).astype(BF16)
+            own_share = misfit[pl.ds(pl.multiple_of(me_c * share, 8), share), :]
+            own_share = own_share - select_dot(pick, change)
+            last_share = select_dot(pick, parts_dir)
         if k + 1 < ITERS:
             wait_bytes(rowbuf.at[k + 1], n_rows, row_recv.at[k + 1])
             adj = get_rows(k + 1)
@@ -289,18 +281,15 @@
             change = alpha * parts_dir
         else:
             solved = [solved[b] + alpha_row * direction[b] for b in range(blocks)]
-            change = change + alpha * parts_dir
+            if k + 1 < ITERS:
+                change = change + alpha * parts_dir
         if k + 1 < ITERS:
             residual = [
                 residual[b] - alpha_row * (adj[b] + DAMPING * direction[b]) for b in range(blocks)
             ]
 
     density_out[...] = to_lanes([density[b] + depth[b] * solved[b] for b in range(blocks)])
-    share = misfit_out.shape[0]
-    wanted = (lax.broadcasted_iota(jnp.int32, (share, n), 0) + me_c * share).astype(F32)
-    pick = (wanted == jnp.transpose(codes)[0:1, :]).astype(F32).astype(BF16)
-    own_share = misfit[pl.ds(pl.multiple_of(me_c * share, 8), share), :]
-    misfit_out[...] = own_share - select_dot(pick, change)
+    misfit_out[...] = own_share - alpha * last_share
 
     wait_bytes(idbuf, n_cols, id_send.at[0])
     for k in range(ITERS):
@@ -322,7 +311,7 @@
     share = data_lanes // n_cols
     mrows = slots * q
     n = n_cols * mrows
-    signs, scale = haar_signs(size)
+    high, low = haar_matrix(size)
     vmem = pl.BlockSpec(memory_space=pltpu.VMEM)
     hbm = pl.BlockSpec(memory_space=pltpu.HBM)
     dma = pltpu.SemaphoreType.DMA
@@ -338,10 +327,10 @@
             pltpu.SMEM((1, slots), jnp.int32),
             pltpu.SMEM((1, slots), jnp.int32),
             pltpu.SMEM((1, slots), jnp.int32),
-            pltpu.VMEM((1, size), F32),
             pltpu.VMEM((cell_lanes, LANES), F32),
             pltpu.VMEM((cell_lanes, LANES), F32),
             pltpu.VMEM((slots, size, size), BF16),
+            pltpu.VMEM((size, size), BF16),
             pltpu.VMEM((size, size), BF16),
             pltpu.VMEM((data_lanes, LANES), F32),
             pltpu.VMEM((data_lanes, LANES), F32),
@@ -359,9 +348,9 @@
             collective_id=0, has_side_effects=True, vmem_limit_bytes=67_043_328
         ),
     )(
-        tile_rows, tile_cols, kept_counts, jnp.asarray(scale),
+        tile_rows, tile_cols, kept_counts,
         depth_weight.reshape(cell_lanes, LANES), density.reshape(cell_lanes, LANES),
-        sensitivity[0], jnp.asarray(signs, BF16),
+        sensitivity[0], jnp.asarray(high), jnp.asarray(low),
         misfit.reshape(data_lanes, LANES), data_weight.reshape(data_lanes, LANES),
     )
     return new_density.reshape(-1), new_misfit.reshape(-1)

time: 46.5 us -> 46.8 us (level)
  no operation moved by 1% of the time
where the time goes in v4:
time: 46.8 us; the launch traced here: 46.6 us
  Pallas kernels  43.3 us (93%)
  local copies, waits for them, and re-layouts  2.65 us (6%)
  between operations  0.64 us (1%)
    pallas_call x1, Pallas kernels, per_device(): pl.pallas_call(functools.partial(kernel, n_rows, n_cols, slots), out_shap...  43.3 us
    unnamed x2, local copies, waits for them, and re-layouts  2.65 us

profile of v4, /device:TPU:0, one launch (start us, length us, event | category | flops | bytes accessed | tf_op | source)
XLA Modules:
  0.0 46.6 jit_solution(17311070617960695394)
XLA Ops:
  0.6 43.3 %shard_map.113 = (f32[8,128]{1,0:T(8,128)}, f32[64,128]{1,0:T(8,128)}) custom-call(s32[1,4]{1,0:T(1,128)} %rows_hbm.1, s32[1,4]{1,0:T(1,128)} %cols_hbm.1, s32[1,4]{1,0:T(1,128)} %kept_hbm.1, f32[8,128]{1,0:T(8,128)} %bitcast.12, f32[8,128]{1,0:T(8,128)} %bitcast.13, bf16[4,512,512]{2,1,0:T(8,128)(2,1)} %bitcast.7, bf16[512,512]{1,0:T(8,128)(2,1)} %constant.4.clone.high_hbm, ...), custom_call_target="tpu_custom_call" | custom-call | tf_op jit(solution)/shard_map/pallas_call | solution.py:318
  43.9 1.3 %copy.14 = f32[1024]{0:T(1024)} copy(f32[1024]{0:T(1024)} %bitcast.11) | data formatting | bytes 8192
  45.2 1.4 %copy.15 = f32[8192]{0:T(1024)} copy(f32[8192]{0:T(1024)} %bitcast.10) | data formatting | bytes 65536

commit v5 on v4

--- a/solution.py
+++ b/solution.py
@@ -141,7 +141,7 @@
         view = buf.at[pl.ds(0, count - 1)]
         pltpu.make_async_copy(view, view, sem).wait()
 
-    for load in loads:
+    for load in loads[:5] + loads[7:9]:
         load.wait()
     sub = lax.broadcasted_iota(jnp.int32, (q, LANES), 0)
     own_weight = jnp.concatenate(
@@ -158,6 +158,19 @@
     lane = lax.broadcasted_iota(jnp.int32, (1, size), 1)
     hits = [[cols_s[0, s] == b for b in range(blocks)] for s in range(slots)]
     depth = to_rows(depth_ref[...], size)
+
+    sums = [jnp.zeros((1, size), F32) for _ in range(blocks)]
+    for s, row in enumerate(to_rows(own_squared * own_misfit, size)):
+        product = jnp.where(lane < kept_s[0, s], nn(row.astype(BF16), tiles[s]), 0.0)
+        for b in range(blocks):
+            sums[b] = sums[b] + jnp.where(hits[s][b], product, 0.0)
+    for b in range(blocks):
+        rowbuf[0, me_r, b : b + 1, :] = sums[b]
+    pl.semaphore_wait(barrier, n_cols + n_rows - 2)
+    send(rowbuf.at[0], "rows", me_r, n_rows, row_send.at[0], row_recv.at[0])
+    send(idbuf, "cols", me_c, n_cols, id_send.at[0], id_recv.at[0])
+    for load in loads[5:7] + loads[9:]:
+        load.wait()
     density = to_rows(density_ref[...], size)
 
     for s in range(slots):
@@ -198,12 +211,14 @@
             sums.append(acc)
         return sums
 
-    put_rows(0, adjoint_blocks((own_squared * own_misfit).astype(BF16).astype(F32)))
-    pl.semaphore_wait(barrier, n_cols + n_rows - 2)
-    send(rowbuf.at[0], "rows", me_r, n_rows, row_send.at[0], row_recv.at[0])
-    send(idbuf, "cols", me_c, n_cols, id_send.at[0], id_recv.at[0])
     wait_bytes(rowbuf.at[0], n_rows, row_recv.at[0])
-    adj = get_rows(0)
+    terms = [split3(row) for row in get_rows(0)]
+    lhs = jnp.concatenate([t[i].astype(F32) for i in range(3) for t in terms], axis=0).astype(BF16)
+    back = nn(lhs, high[...]) + nn(lhs, low[...])
+    adj = []
+    for b in range(blocks):
+        at = [back[i * blocks + b : i * blocks + b + 1] for i in range(3)]
+        adj.append(depth[b] * (at[0] + (at[1] + at[2])))
     residual = [adj[b] - DAMPING * density[b] for b in range(blocks)]
     direction = None
     solved = None
@@ -217,11 +232,11 @@
             dots.append(total([residual[b] * direction[b] for b in range(blocks)]))
         else:
             dots.append(jnp.zeros((1, 1), F32))
+        colbuf[k, me_c, :, :] = forward_parts(residual).astype(BF16)
         for i in range(2):
             dotbuf[k, me_c, i : i + 1, :] = jnp.broadcast_to(dots[i], (1, LANES))
+        send(colbuf.at[k], "cols", me_c, n_cols, col_send.at[k], col_recv.at[k])
         send(dotbuf.at[k], "cols", me_c, n_cols, dot_send.at[k], dot_recv.at[k])
-        colbuf[k, me_c, :, :] = forward_parts(residual).astype(BF16)
-        send(colbuf.at[k], "cols", me_c, n_cols, col_send.at[k], col_recv.at[k])
         if k == 0:
             wait_bytes(idbuf, n_cols, id_recv.at[0])
             codes = idbuf[:, mrows : 2 * mrows, :].reshape(n, LANES)

time: 46.8 us -> 45.8 us (0.979)
  Pallas kernels: 43.3 us -> 42.3 us
    pallas_call x1, Pallas kernels: 43.3 us -> 42.3 us  [per_device(): pl.pallas_call(functools.partial(kernel, n_rows, n_cols, slots), out_shap...]
where the time goes in v5:
time: 45.8 us; the launch traced here: 45.6 us
  Pallas kernels  42.3 us (92%)
  local copies, waits for them, and re-layouts  2.65 us (6%)
  between operations  0.64 us (1%)
    pallas_call x1, Pallas kernels, per_device(): pl.pallas_call(functools.partial(kernel, n_rows, n_cols, slots), out_shap...  42.3 us
    unnamed x2, local copies, waits for them, and re-layouts  2.65 us

profile of v5, /device:TPU:0, one launch (start us, length us, event | category | flops | bytes accessed | tf_op | source)
XLA Modules:
  0.0 45.6 jit_solution(10706893166002490007)
XLA Ops:
  0.6 42.3 %shard_map.113 = (f32[8,128]{1,0:T(8,128)}, f32[64,128]{1,0:T(8,128)}) custom-call(s32[1,4]{1,0:T(1,128)} %rows_hbm.1, s32[1,4]{1,0:T(1,128)} %cols_hbm.1, s32[1,4]{1,0:T(1,128)} %kept_hbm.1, f32[8,128]{1,0:T(8,128)} %bitcast.12, f32[8,128]{1,0:T(8,128)} %bitcast.13, bf16[4,512,512]{2,1,0:T(8,128)(2,1)} %bitcast.7, bf16[512,512]{1,0:T(8,128)(2,1)} %constant.4.clone.high_hbm, ...), custom_call_target="tpu_custom_call" | custom-call | tf_op jit(solution)/shard_map/pallas_call | solution.py:333
  43.0 1.3 %copy.14 = f32[1024]{0:T(1024)} copy(f32[1024]{0:T(1024)} %bitcast.11) | data formatting | bytes 8192
  44.2 1.4 %copy.15 = f32[8192]{0:T(1024)} copy(f32[8192]{0:T(1024)} %bitcast.10) | data formatting | bytes 65536

commit v6 on v5

--- a/solution.py
+++ b/solution.py
@@ -235,8 +235,8 @@
         colbuf[k, me_c, :, :] = forward_parts(residual).astype(BF16)
         for i in range(2):
             dotbuf[k, me_c, i : i + 1, :] = jnp.broadcast_to(dots[i], (1, LANES))
-        send(colbuf.at[k], "cols", me_c, n_cols, col_send.at[k], col_recv.at[k])
-        send(dotbuf.at[k], "cols", me_c, n_cols, dot_send.at[k], dot_recv.at[k])
+        send(colbuf.at[k], "cols", me_c, n_cols, col_send.at[0], col_recv.at[k])
+        send(dotbuf.at[k], "cols", me_c, n_cols, dot_send.at[0], dot_recv.at[k])
         if k == 0:
             wait_bytes(idbuf, n_cols, id_recv.at[0])
             codes = idbuf[:, mrows : 2 * mrows, :].reshape(n, LANES)
@@ -272,9 +272,9 @@
             image_ref[...] = image
             own_image = image_ref[pl.ds(pl.multiple_of(me_c * mrows, mrows), mrows), :]
             put_rows(k + 1, adjoint_blocks(own_squared * own_image))
-            send(rowbuf.at[k + 1], "rows", me_r, n_rows, row_send.at[k + 1], row_recv.at[k + 1])
+            send(rowbuf.at[k + 1], "rows", me_r, n_rows, row_send.at[0], row_recv.at[k + 1])
         curvbuf[k, me_r, :, :] = jnp.broadcast_to(curv_part, (1, LANES))
-        send(curvbuf.at[k], "rows", me_r, n_rows, curv_send.at[k], curv_recv.at[k])
+        send(curvbuf.at[k], "rows", me_r, n_rows, curv_send.at[0], curv_recv.at[k])
         if k + 1 == ITERS:
             share = misfit_out.shape[0]
             wanted = (lax.broadcasted_iota(jnp.int32, (share, n), 0) + me_c * share).astype(F32)
@@ -307,11 +307,12 @@
     misfit_out[...] = own_share - alpha * last_share
 
     wait_bytes(idbuf, n_cols, id_send.at[0])
-    for k in range(ITERS):
-        wait_bytes(colbuf.at[k], n_cols, col_send.at[k])
-        wait_bytes(dotbuf.at[k], n_cols, dot_send.at[k])
-        wait_bytes(rowbuf.at[k], n_rows, row_send.at[k])
-        wait_bytes(curvbuf.at[k], n_rows, curv_send.at[k])
+    for buf, count, sem in (
+        (colbuf, n_cols, col_send), (dotbuf, n_cols, dot_send),
+        (rowbuf, n_rows, row_send), (curvbuf, n_rows, curv_send),
+    ):
+        view = buf.at[:, pl.ds(0, count - 1)]
+        pltpu.make_async_copy(view, view, sem.at[0]).wait()
 
 
 def per_device(
@@ -356,8 +357,8 @@
             pltpu.VMEM((ITERS, n_rows, 1, LANES), F32),
             pltpu.VMEM((n, LANES), F32),
             pltpu.VMEM((n, n), BF16),
-            dma((10,)), dma((1,)), dma((1,)), dma((ITERS,)), dma((ITERS,)),
-            dma((ITERS,)), dma((ITERS,)), dma((ITERS,)), dma((ITERS,)), dma((ITERS,)), dma((ITERS,)),
+            dma((10,)), dma((1,)), dma((1,)), dma((1,)), dma((ITERS,)),
+            dma((1,)), dma((ITERS,)), dma((1,)), dma((ITERS,)), dma((1,)), dma((ITERS,)),
         ],
         compiler_params=pltpu.CompilerParams(
             collective_id=0, has_side_effects=True, vmem_limit_bytes=67_043_328

time: 45.8 us -> 45.7 us (level)
  no operation moved by 1% of the time
where the time goes in v6:
time: 45.7 us; the launch traced here: 45.5 us
  Pallas kernels  42.2 us (92%)
  local copies, waits for them, and re-layouts  2.65 us (6%)
  between operations  0.64 us (1%)
    pallas_call x1, Pallas kernels, per_device(): pl.pallas_call(functools.partial(kernel, n_rows, n_cols, slots), out_shap...  42.2 us
    unnamed x2, local copies, waits for them, and re-layouts  2.65 us

profile of v6, /device:TPU:0, one launch (start us, length us, event | category | flops | bytes accessed | tf_op | source)
XLA Modules:
  0.0 45.5 jit_solution(7073201310363779344)
XLA Ops:
  0.6 42.2 %shard_map.113 = (f32[8,128]{1,0:T(8,128)}, f32[64,128]{1,0:T(8,128)}) custom-call(s32[1,4]{1,0:T(1,128)} %rows_hbm.1, s32[1,4]{1,0:T(1,128)} %cols_hbm.1, s32[1,4]{1,0:T(1,128)} %kept_hbm.1, f32[8,128]{1,0:T(8,128)} %bitcast.12, f32[8,128]{1,0:T(8,128)} %bitcast.13, bf16[4,512,512]{2,1,0:T(8,128)(2,1)} %bitcast.7, bf16[512,512]{1,0:T(8,128)(2,1)} %constant.4.clone.high_hbm, ...), custom_call_target="tpu_custom_call" | custom-call | tf_op jit(solution)/shard_map/pallas_call | solution.py:334
  42.8 1.3 %copy.14 = f32[1024]{0:T(1024)} copy(f32[1024]{0:T(1024)} %bitcast.11) | data formatting | bytes 8192
  44.1 1.4 %copy.15 = f32[8192]{0:T(1024)} copy(f32[8192]{0:T(1024)} %bitcast.10) | data formatting | bytes 65536
